TPU v7x, 32 devices: a whole 2x2x4 slice. The times are simulated.
32 devices in a mesh: gx: 2 (over y), gy: 4 (over x, core), gz: 4 (over z).
Axes of the slice: x: 2, y: 2, z: 4, core: 2. Of those that a mesh axis runs over, the one named last changes fastest.
Arguments:
- direction: float32 [3, 32, 32, 512], P(None, 'gx', 'gy', 'gz'), may hold values from -6 to 6
- base_flow: bfloat16 [2, 3, 32, 32, 512], P(None, None, 'gx', 'gy', 'gz'), may hold values from -4 to 4
- local_inv: float32 [32, 16], P('gx'), may hold values from -1.5 to 1.5
- couple_in: float32 [4, 16], P('gx'), may hold values from -1.5 to 1.5
- couple_out: float32 [32, 2], P('gx'), may hold values from -4 to 4
- schur_inv: float32 [4, 4], replicated, may hold values from -3 to 3
- plane_x: int32 [8], replicated, may hold values from 0 to 31, as said below
- slot_plane: int32 [8], replicated, may hold values from 0 to 7, each once
- window_inv: float32 [8, 4, 4, 16, 16], P('gx', 'gy', 'gz'), may hold values from -4 to 20
Outputs:
- hess_vec: float32 [3, 32, 32, 512], P(None, 'gx', 'gy', 'gz')
Inputs may be any that keep to these rules, and one draw needn't show every extreme that they name: `plane_x`: each plane lies on a streamwise cell of the grid; the planes lie on distinct cells; at most 8 of them lie in the cells of one index d of gx (cells d*16 to d*16 + 15), and some index holds exactly 8.
All inputs are finite; a program needn't handle non-finite values.
Results may differ from a plain program's by a relative error of at most 0.0003.
Values sent between devices are 32-bit elements; how exact they have to be, the bound alone decides.
A program may use at most 64 MiB of HBM per device.

v0:
```python
import jax
import jax.numpy as jnp
from jax import lax
from jax.sharding import PartitionSpec as P

WIN = 8
time_step = 0.15
high = lax.Precision.HIGHEST


def extended(cells, sides, width, closed):
    for axis, dim in sides:
        count = lax.axis_size(axis)
        ends = count if closed else count - 1
        head = lax.slice_in_dim(cells, 0, width, axis=dim)
        tail = lax.slice_in_dim(cells, cells.shape[dim] - width, cells.shape[dim], axis=dim)
        cells = jnp.concatenate(
            [
                lax.ppermute(tail, axis, [(i, (i + 1) % count) for i in range(ends)]),
                cells,
                lax.ppermute(head, axis, [((i + 1) % count, i) for i in range(ends)]),
            ],
            axis=dim,
        )
    return cells


def stencil_x(field):
    length = field.shape[1]
    padded = extended(field, (("gx", 1),), 2, False)
    near_diff = padded[:, 3 : length + 3] - padded[:, 1 : length + 1]
    far_diff = padded[:, 4 : length + 4] - padded[:, 0:length]
    return 7.0 / 9.0 * near_diff + 1.0 / 36.0 * far_diff


def cross_padded(field):
    return extended(field, (("gy", 2), ("gz", 3)), 3, True)


def sixth_order(minus_one, plus_one, minus_two, plus_two, minus_three, plus_three):
    return (
        45.0 * (plus_one - minus_one) - 9.0 * (plus_two - minus_two) + (plus_three - minus_three)
    ) / 60.0


def along_y(padded):
    height = padded.shape[2] - 6
    middle = padded[:, :, :, 3 : padded.shape[3] - 3]

    def taken(offset):
        return middle[:, :, 3 + offset : 3 + offset + height]

    return sixth_order(taken(-1), taken(1), taken(-2), taken(2), taken(-3), taken(3))


def along_z(padded):
    breadth = padded.shape[3] - 6
    middle = padded[:, :, 3 : padded.shape[2] - 3, :]

    def taken(offset):
        return middle[:, :, :, 3 + offset : 3 + offset + breadth]

    return sixth_order(taken(-1), taken(1), taken(-2), taken(2), taken(-3), taken(3))


def interface_sum(edge_values, weight_cols):
    return jnp.einsum(
        "ma,mcyz->acyz",
        weight_cols,
        lax.all_gather(edge_values, "gx", axis=0, tiled=True),
        precision=high,
    )


def local(
    direction,
    base_flow,
    local_inv,
    couple_in,
    couple_out,
    schur_inv,
    plane_x,
    slot_plane,
    window_inv,
):
    gx_index = lax.axis_index("gx")
    holders = lax.axis_size("gx")
    x_cells = direction.shape[1]
    planes = plane_x.shape[0]
    owned_slots = window_inv.shape[0]
    window_count = window_inv.shape[3]
    hold_most = min(planes, 3 * owned_slots)
    own_rows = lax.dynamic_slice_in_dim(schur_inv, 2 * gx_index, 2, 0)
    own_cols = lax.dynamic_slice_in_dim(schur_inv, 2 * gx_index, 2, 1)

    def solve_x(rhs):
        local_part = jnp.einsum("ij,cjyz->ciyz", local_inv, rhs, precision=high)
        edge_values = jnp.einsum("kj,cjyz->kcyz", couple_in, rhs, precision=high)
        solved = interface_sum(edge_values, jnp.transpose(own_rows))
        return local_part + jnp.einsum("ik,kcyz->ciyz", couple_out, solved, precision=high)

    def solve_x_adjoint(grad_in):
        local_part = jnp.einsum("ji,cjyz->ciyz", local_inv, grad_in, precision=high)
        edge_values = jnp.einsum("ik,ciyz->kcyz", couple_out, grad_in, precision=high)
        solved = interface_sum(edge_values, own_cols)
        return local_part + jnp.einsum("ki,kcyz->ciyz", couple_in, solved, precision=high)

    owner_of = plane_x // x_cells
    device_hot = (owner_of[None, :] == jnp.arange(holders, dtype=jnp.int32)[:, None]).astype(
        jnp.int32
    )
    ranks = jnp.cumsum(device_hot, axis=1) - 1
    slot_range = jnp.arange(hold_most, dtype=jnp.int32)[None, :, None]
    pick_all = ((device_hot[:, None, :] == 1) & (ranks[:, None, :] == slot_range)).astype(
        jnp.float32
    )
    pick_own = lax.dynamic_index_in_dim(pick_all, gx_index, 0, keepdims=False)
    local_x = plane_x - gx_index * x_cells
    slot_x = jnp.sum(jnp.where(pick_own > 0, local_x[None, :], 0), axis=1)
    filled = jnp.sum(pick_own, axis=1) > 0
    cell_range = jnp.arange(x_cells, dtype=jnp.int32)[None, :]
    select = (filled[:, None] & (slot_x[:, None] == cell_range)).astype(jnp.float32)
    plane_slot = (slot_plane[:, None] == jnp.arange(planes, dtype=jnp.int32)[None, :]).astype(
        jnp.float32
    )
    route = jnp.dot(pick_own, jnp.transpose(plane_slot), precision=high)
    inverse_here = window_inv.reshape(owned_slots, window_count, window_count)

    def windows_of(state):
        plane_rows = jnp.einsum("sx,cxyz->scyz", select, state, precision=high)
        return plane_rows.reshape(
            plane_rows.shape[0], 3, plane_rows.shape[2], plane_rows.shape[3] // WIN, WIN
        ).mean(axis=4)

    def spread_back(weighted):
        expanded = jnp.repeat(weighted, WIN, axis=3) / WIN
        return jnp.einsum("sx,scyz->cxyz", select, expanded, precision=high)

    every_inv = lax.all_gather(inverse_here, "gx", axis=0, tiled=True)
    held_inv = jnp.einsum("sj,jab->sab", route, every_inv, precision=high)

    def observe(state):
        weighted = jnp.einsum("sab,scyb->scya", held_inv, windows_of(state), precision=high)
        return spread_back(weighted)

    def tangent(state, step_base):
        velocity = step_base.astype(jnp.float32)
        slope_x = solve_x(stencil_x(state))
        padded = cross_padded(state)
        return state - time_step * (
            velocity[0] * slope_x + velocity[1] * along_y(padded) + velocity[2] * along_z(padded)
        )

    def adjoint(state, step_base):
        velocity = step_base.astype(jnp.float32)
        pulled = stencil_x(solve_x_adjoint(velocity[0] * state))
        padded = cross_padded(jnp.concatenate([velocity[1] * state, velocity[2] * state], axis=0))
        return state + time_step * (pulled + along_y(padded[:3]) + along_z(padded[3:]))

    state_one = tangent(direction, base_flow[0])
    state_two = tangent(state_one, base_flow[1])
    adjoint_two = observe(state_two)
    adjoint_one = adjoint(adjoint_two, base_flow[1]) + observe(state_one)
    return adjoint(adjoint_one, base_flow[0]) + direction


def solution(mesh):
    return jax.shard_map(
        local,
        mesh=mesh,
        in_specs=(
            P(None, "gx", "gy", "gz"),
            P(None, None, "gx", "gy", "gz"),
            P("gx", None),
            P("gx", None),
            P("gx", None),
            P(),
            P(),
            P(),
            P("gx", "gy", "gz", None, None),
        ),
        out_specs=P(None, "gx", "gy", "gz"),
        check_vma=False,
    )
```

profile of v0, /device:TPU:0, one launch (start us, length us, event | category | flops | bytes accessed | tf_op | source)
XLA Modules:
  0.0 129.9 jit_solution(2365292226690273208)
XLA Ops:
  0.0 1.0 copy.84
  1.6 2.0 %collective-permute-start.2 = (f32[3,16,3,128]{3,1,2,0:T(8,128)S(1)}, f32[3,16,3,128]{3,1,2,0:T(8,128)S(1)}, u32[]{:S(2)}, u32[]{:S(2)}) collective-permute-start(f32[3,16,3,128]{3,1,2,0:T(8,128)S(1)} %get-tuple-element.51), channel_id=1, source_target_pairs={{4,0},{8,4},{12,8},{0,12},{5,1},{9,5},{13,9},{1,13},{6,2},{10,6},{... | collective-permute-start | bytes 221192 | tf_op jit(solution)/shard_map/ppermute | solution.py:21
  3.6 4.2 %collective-permute-start.1 = (f32[3,2,8,128]{3,1,2,0:T(2,128)S(1)}, f32[3,2,8,128]{3,1,2,0:T(2,128)S(1)}, u32[]{:S(2)}, u32[]{:S(2)}) collective-permute-start(f32[3,2,8,128]{3,1,2,0:T(2,128)S(1)} %get-tuple-element.44), channel_id=1, source_target_pairs={{0,16},{1,17},{2,18},{3,19},{4,20},{5,21},{6,22},{7,23},{8,24},{9,... | collective-permute-start | bytes 73736 | tf_op jit(solution)/shard_map/ppermute | solution.py:19
  7.8 1.3 collective-permute-start
  9.1 1.0 slice_convert_fusion
  12.0 5.2 %all-gather = f32[8,1,1,16,16]{4,3,2,1,0:T(8,128)S(1)} all-gather(f32[4,1,1,16,16]{4,3,2,1,0:T(8,128)S(1)} %copy-done.4), channel_id=2, replica_groups=mesh['gx'=2,'gy'=4,'gz'=4] {'gx'}, dimensions={0}, use_global_device_ids=true | all-gather | bytes 12288 | tf_op jit(solution)/shard_map/all_gather | solution.py:139
  18.0 1.6 %collective-permute-start.5 = (f32[3,16,14,3]{3,1,2,0:T(8,128)S(1)}, f32[3,16,14,3]{3,1,2,0:T(8,128)S(1)}, u32[]{:S(2)}, u32[]{:S(2)}) collective-permute-start(f32[3,16,14,3]{3,1,2,0:T(8,128)S(1)} %get-tuple-element.20), channel_id=1, source_target_pairs={{0,1},{1,2},{2,3},{3,0},{4,5},{5,6},{6,7},{7,4},{8,9},{9,10},{10,1... | collective-permute-start | bytes 24200 | tf_op jit(solution)/shard_map/ppermute | solution.py:19
  19.6 2.2 %collective-permute-start.4 = (f32[3,16,14,3]{3,1,2,0:T(8,128)S(1)}, f32[3,16,14,3]{3,1,2,0:T(8,128)S(1)}, u32[]{:S(2)}, u32[]{:S(2)}) collective-permute-start(f32[3,16,14,3]{3,1,2,0:T(8,128)S(1)} %get-tuple-element.19), channel_id=1, source_target_pairs={{1,0},{2,1},{3,2},{0,3},{5,4},{6,5},{7,6},{4,7},{9,8},{10,9},{11,1... | collective-permute-start | bytes 24200 | tf_op jit(solution)/shard_map/ppermute | solution.py:21
  22.6 4.5 %all_gather.15 = f32[4,3,8,128]{3,2,1,0:T(8,128)S(1)} all-gather(f32[2,3,8,128]{3,2,1,0:T(8,128)S(1)} %copy.75), channel_id=1, replica_groups=mesh['gx'=2,'gy'=4,'gz'=4] {'gx'}, dimensions={0}, use_global_device_ids=true | all-gather | bytes 73728 | tf_op jit(solution)/shard_map/all_gather | solution.py:70
  27.3 3.5 %collective-permute-done.5 = f32[3,16,14,3]{3,1,2,0:T(8,128)S(1)} collective-permute-done((f32[3,16,14,3]{3,1,2,0:T(8,128)S(1)}, f32[3,16,14,3]{3,1,2,0:T(8,128)S(1)}, u32[]{:S(2)}, u32[]{:S(2)}) %collective-permute-start.5) | collective-permute-done | bytes 8096 | tf_op jit(solution)/shard_map/ppermute | solution.py:19
  30.8 4.3 %collective-permute-done.4 = f32[3,16,14,3]{3,1,2,0:T(8,128)S(1)} collective-permute-done((f32[3,16,14,3]{3,1,2,0:T(8,128)S(1)}, f32[3,16,14,3]{3,1,2,0:T(8,128)S(1)}, u32[]{:S(2)}, u32[]{:S(2)}) %collective-permute-start.4) | collective-permute-done | bytes 8096 | tf_op jit(solution)/shard_map/ppermute | solution.py:21
  35.1 0.8 fusion.90
  36.2 0.8 reshape.79
  37.0 3.7 %collective-permute-start.7 = (f32[3,2,8,128]{3,1,2,0:T(2,128)S(1)}, f32[3,2,8,128]{3,1,2,0:T(2,128)S(1)}, u32[]{:S(2)}, u32[]{:S(2)}) collective-permute-start(f32[3,2,8,128]{3,1,2,0:T(2,128)S(1)} %get-tuple-element.42), channel_id=1, source_target_pairs={{0,16},{1,17},{2,18},{3,19},{4,20},{5,21},{6,22},{7,23},{8,24},{9,... | collective-permute-start | bytes 73736 | tf_op jit(solution)/shard_map/ppermute | solution.py:19
  40.7 1.3 collective-permute-start.6
  43.3 0.8 div.55
  44.1 1.7 %collective-permute-start.8 = (f32[3,16,3,128]{3,1,2,0:T(8,128)S(1)}, f32[3,16,3,128]{3,1,2,0:T(8,128)S(1)}, u32[]{:S(2)}, u32[]{:S(2)}) collective-permute-start(f32[3,16,3,128]{3,1,2,0:T(8,128)S(1)} %get-tuple-element.37), channel_id=1, source_target_pairs={{4,0},{8,4},{12,8},{0,12},{5,1},{9,5},{13,9},{1,13},{6,2},{10,6},{... | collective-permute-start | bytes 221192 | tf_op jit(solution)/shard_map/ppermute | solution.py:21
  47.1 4.5 %all_gather.16 = f32[4,3,8,128]{3,2,1,0:T(8,128)S(1)} all-gather(f32[2,3,8,128]{3,2,1,0:T(8,128)S(1)} %copy.86), channel_id=1, replica_groups=mesh['gx'=2,'gy'=4,'gz'=4] {'gx'}, dimensions={0}, use_global_device_ids=true | all-gather | bytes 73728 | tf_op jit(solution)/shard_map/all_gather | solution.py:70
  52.1 1.2 collective-permute-start.11
  53.3 2.7 %collective-permute-start.10 = (f32[3,16,14,3]{3,1,2,0:T(8,128)S(1)}, f32[3,16,14,3]{3,1,2,0:T(8,128)S(1)}, u32[]{:S(2)}, u32[]{:S(2)}) collective-permute-start(f32[3,16,14,3]{3,1,2,0:T(8,128)S(1)} %get-tuple-element.17), channel_id=1, source_target_pairs={{1,0},{2,1},{3,2},{0,3},{5,4},{6,5},{7,6},{4,7},{9,8},{10,9},{11,1... | collective-permute-start | bytes 24200 | tf_op jit(solution)/shard_map/ppermute | solution.py:21
  56.3 8.5 %collective-permute-done.11 = f32[3,16,14,3]{3,1,2,0:T(8,128)S(1)} collective-permute-done((f32[3,16,14,3]{3,1,2,0:T(8,128)S(1)}, f32[3,16,14,3]{3,1,2,0:T(8,128)S(1)}, u32[]{:S(2)}, u32[]{:S(2)}) %collective-permute-start.11) | collective-permute-done | bytes 8096 | tf_op jit(solution)/shard_map/ppermute | solution.py:19
  64.9 3.5 %collective-permute-done.10 = f32[3,16,14,3]{3,1,2,0:T(8,128)S(1)} collective-permute-done((f32[3,16,14,3]{3,1,2,0:T(8,128)S(1)}, f32[3,16,14,3]{3,1,2,0:T(8,128)S(1)}, u32[]{:S(2)}, u32[]{:S(2)}) %collective-permute-start.10) | collective-permute-done | bytes 8096 | tf_op jit(solution)/shard_map/ppermute | solution.py:21
  68.4 0.8 fusion.102
  69.2 0.8 reshape.77
  71.3 0.8 div.50
  73.7 4.6 %all_gather.18 = f32[4,3,8,128]{3,2,1,0:T(8,128)S(1)} all-gather(f32[2,3,8,128]{3,2,1,0:T(8,128)S(1)} %copy.96), channel_id=1, replica_groups=mesh['gx'=2,'gy'=4,'gz'=4] {'gx'}, dimensions={0}, use_global_device_ids=true | all-gather | bytes 73728 | tf_op jit(solution)/shard_map/all_gather | solution.py:70
  79.0 3.7 %collective-permute-start.13 = (f32[3,2,8,128]{3,1,2,0:T(2,128)S(1)}, f32[3,2,8,128]{3,1,2,0:T(2,128)S(1)}, u32[]{:S(2)}, u32[]{:S(2)}) collective-permute-start(f32[3,2,8,128]{3,1,2,0:T(2,128)S(1)} %get-tuple-element.34), channel_id=1, source_target_pairs={{0,16},{1,17},{2,18},{3,19},{4,20},{5,21},{6,22},{7,23},{8,24},{9,... | collective-permute-start | bytes 73736 | tf_op jit(solution)/shard_map/ppermute | solution.py:19
  82.6 1.3 collective-permute-start.12
  85.0 1.0 collective-permute-start.17
  86.7 3.1 %collective-permute-start.16 = (f32[6,16,14,3]{2,1,3,0:T(8,128)S(1)}, f32[6,16,14,3]{2,1,3,0:T(8,128)}, u32[]{:S(2)}, u32[]{:S(2)}) collective-permute-start(f32[6,16,14,3]{2,1,3,0:T(8,128)S(1)} %copy.100), channel_id=1, source_target_pairs={{1,0},{2,1},{3,2},{0,3},{5,4},{6,5},{7,6},{4,7},{9,8},{10,9},{11,1... | collective-permute-start | bytes 48392 | tf_op jit(solution)/shard_map/ppermute | solution.py:21
  89.8 1.1 pad_maximum_fusion.2
  90.9 2.9 %collective-permute-done.17 = f32[6,16,14,3]{2,1,3,0:T(8,128)S(1)} collective-permute-done((f32[6,16,14,3]{2,1,3,0:T(8,128)S(1)}, f32[6,16,14,3]{2,1,3,0:T(8,128)S(1)}, u32[]{:S(2)}, u32[]{:S(2)}) %collective-permute-start.17) | collective-permute-done | bytes 16160 | tf_op jit(solution)/shard_map/ppermute | solution.py:19
  93.8 0.8 copy.103
  94.5 1.0 collective-permute-done.16
  95.5 1.7 %copy.101 = f32[6,16,14,3]{3,1,2,0:T(8,128)S(1)} copy(f32[6,16,14,3]{2,1,3,0:T(8,128)} %collective-permute-done.16) | data formatting | bytes 32256 | tf_op jit(solution)/shard_map/ppermute | solution.py:21
  97.8 2.1 %broadcast_multiply_fusion.1 = (f32[3,16,8,128]{3,1,2,0:T(8,128)S(1)}, f32[3,16,8,128]{3,1,2,0:T(8,128)S(1)}, f32[3,16,8,128]{3,1,2,0:T(8,128)S(1)}) fusion(f32[16,8,128]{2,0,1:T(8,128)S(1)} %copy-done.3, f32[16,8,128]{2,0,1:T(8,128)} %copy.111, s32[8]{0:T(128)S(1)} %copy-done.10, pred[8]{0:T(512)(128)(4,1)S(1)} %copy-done.12, ...), kind=kOutput, calls=%fused_computation.209 | convolution fusion | flops 7471360 | bytes 3161640 | tf_op jit(solution)/shard_map/sx,scyz->cxyz/dot_general | solution.py:137
  100.6 4.8 %all_gather.19 = f32[4,3,8,128]{3,2,1,0:T(8,128)S(1)} all-gather(f32[2,3,8,128]{3,2,1,0:T(8,128)S(1)} %copy.108), channel_id=1, replica_groups=mesh['gx'=2,'gy'=4,'gz'=4] {'gx'}, dimensions={0}, use_global_device_ids=true | all-gather | bytes 73728 | tf_op jit(solution)/shard_map/all_gather | solution.py:70
  107.4 4.5 %collective-permute-start.19 = (f32[3,2,8,128]{3,1,2,0:T(2,128)}, f32[3,2,8,128]{3,1,2,0:T(2,128)}, u32[]{:S(2)}, u32[]{:S(2)}) collective-permute-start(f32[3,2,8,128]{3,1,2,0:T(2,128)} %get-tuple-element.27), channel_id=1, source_target_pairs={{0,16},{1,17},{2,18},{3,19},{4,20},{5,21},{6,22},{7,23},{8,24},{9,... | collective-permute-start | bytes 73736 | tf_op jit(solution)/shard_map/ppermute | solution.py:19
  111.9 1.3 collective-permute-start.18
  113.6 1.4 %copy.114 = f32[6,16,14,3]{2,1,3,0:T(8,128)} copy(f32[6,16,14,3]{3,1,2,0:T(8,128)S(1)} %get-tuple-element.6) | data formatting | bytes 32256 | tf_op jit(solution)/shard_map/slice | solution.py:16
  115.0 1.1 collective-permute-start.23
  116.8 2.8 %collective-permute-start.22 = (f32[6,16,14,3]{2,1,3,0:T(8,128)S(1)}, f32[6,16,14,3]{2,1,3,0:T(8,128)}, u32[]{:S(2)}, u32[]{:S(2)}) collective-permute-start(f32[6,16,14,3]{2,1,3,0:T(8,128)S(1)} %copy.112), channel_id=1, source_target_pairs={{1,0},{2,1},{3,2},{0,3},{5,4},{6,5},{7,6},{4,7},{9,8},{10,9},{11,1... | collective-permute-start | bytes 48392 | tf_op jit(solution)/shard_map/ppermute | solution.py:21
  119.6 4.1 %collective-permute-done.23 = f32[6,16,14,3]{2,1,3,0:T(8,128)S(1)} collective-permute-done((f32[6,16,14,3]{2,1,3,0:T(8,128)}, f32[6,16,14,3]{2,1,3,0:T(8,128)S(1)}, u32[]{:S(2)}, u32[]{:S(2)}) %collective-permute-start.23) | collective-permute-done | bytes 16160 | tf_op jit(solution)/shard_map/ppermute | solution.py:19
  123.7 0.8 copy.115
  124.5 1.0 collective-permute-done.22
  125.5 1.7 %copy.113 = f32[6,16,14,3]{3,1,2,0:T(8,128)S(1)} copy(f32[6,16,14,3]{2,1,3,0:T(8,128)} %collective-permute-done.22) | data formatting | bytes 32256 | tf_op jit(solution)/shard_map/ppermute | solution.py:21
  127.2 1.9 %fusion.30 = f32[3,16,8,128]{3,1,2,0:T(8,128)S(1)} fusion(f32[3,16,8,128]{3,1,2,0:T(8,128)S(1)} %get-tuple-element.62, f32[3,2,8,128]{3,1,2,0:T(2,128)} %collective-permute-done.19, f32[3,16,8,128]{3,1,2,0:T(8,128)} %copy-done.2, f32[3,2,8,128]{3,1,2,0:T(2,128)} %collective-permute-done.18, f32[6,16,14,3]{3,1,2,0:T(8,128)S(1)} %copy.115, ...), kind=kLoop, calls=%fused_computation.73 | loop fusion | flops 2654208 | bytes 2735616 | tf_op jit(solution)/shard_map/add | solution.py:164
  129.1 0.7 copy.117
  (132 shorter events, 17.3 us)
Async XLA Ops:
  0.0 22.0 %copy-start = (f32[16,16]{1,0:T(8,128)S(1)}, f32[16,16]{1,0:T(8,128)}, u32[]{:S(2)}) copy-start(f32[16,16]{1,0:T(8,128)} %param.11) | copy-start | bytes 3076
  0.0 11.4 %copy-start.13 = (s32[8]{0:T(128)S(1)}, s32[8]{0:T(128)}, u32[]{:S(2)}) copy-start(s32[8]{0:T(128)} %param.15) | copy-start | bytes 100
  1.0 10.8 %copy-start.16 = (s32[8]{0:T(128)S(1)}, s32[8]{0:T(128)}, u32[]{:S(2)}) copy-start(s32[8]{0:T(128)} %param.16) | copy-start | bytes 100
  1.0 11.0 %copy-start.4 = (f32[4,1,1,16,16]{4,3,2,1,0:T(8,128)S(1)}, f32[4,1,1,16,16]{4,3,2,1,0:T(8,128)}, u32[]{:S(2)}) copy-start(f32[4,1,1,16,16]{4,3,2,1,0:T(8,128)} %param.17) | copy-start | bytes 12292
  1.0 16.6 %collective-permute-start.3 = (f32[3,16,3,128]{3,1,2,0:T(8,128)S(1)}, f32[3,16,3,128]{3,1,2,0:T(8,128)S(1)}, u32[]{:S(2)}, u32[]{:S(2)}) collective-permute-start(f32[3,16,3,128]{3,1,2,0:T(8,128)S(1)} %get-tuple-element.52), channel_id=1, source_target_pairs={{0,4},{4,8},{8,12},{12,0},{1,5},{5,9},{9,13},{13,1},{2,6},{6,10},{... | collective-permute-start | bytes 221192 | tf_op jit(solution)/shard_map/ppermute | solution.py:19
  1.6 16.2 %collective-permute-start.2 = (f32[3,16,3,128]{3,1,2,0:T(8,128)S(1)}, f32[3,16,3,128]{3,1,2,0:T(8,128)S(1)}, u32[]{:S(2)}, u32[]{:S(2)}) collective-permute-start(f32[3,16,3,128]{3,1,2,0:T(8,128)S(1)} %get-tuple-element.51), channel_id=1, source_target_pairs={{4,0},{8,4},{12,8},{0,12},{5,1},{9,5},{13,9},{1,13},{6,2},{10,6},{... | collective-permute-start | bytes 221192 | tf_op jit(solution)/shard_map/ppermute | solution.py:21
  3.6 18.3 %collective-permute-start.1 = (f32[3,2,8,128]{3,1,2,0:T(2,128)S(1)}, f32[3,2,8,128]{3,1,2,0:T(2,128)S(1)}, u32[]{:S(2)}, u32[]{:S(2)}) collective-permute-start(f32[3,2,8,128]{3,1,2,0:T(2,128)S(1)} %get-tuple-element.44), channel_id=1, source_target_pairs={{0,16},{1,17},{2,18},{3,19},{4,20},{5,21},{6,22},{7,23},{8,24},{9,... | collective-permute-start | bytes 73736 | tf_op jit(solution)/shard_map/ppermute | solution.py:19
  7.8 14.1 %collective-permute-start = (f32[3,2,8,128]{3,1,2,0:T(2,128)S(1)}, f32[3,2,8,128]{3,1,2,0:T(2,128)S(1)}, u32[]{:S(2)}, u32[]{:S(2)}) collective-permute-start(f32[3,2,8,128]{3,1,2,0:T(2,128)S(1)} %get-tuple-element.43), channel_id=1, source_target_pairs={{16,0},{17,1},{18,2},{19,3},{20,4},{21,5},{22,6},{23,7},{24,8},{25... | collective-permute-start | bytes 73736 | tf_op jit(solution)/shard_map/ppermute | solution.py:21
  10.0 7.6 %copy-start.1 = (f32[3,16,8,128]{3,2,1,0:T(8,128)S(1)}, f32[3,16,8,128]{3,2,1,0:T(8,128)}, u32[]{:S(2)}) copy-start(f32[3,16,8,128]{3,2,1,0:T(8,128)} %param.9) | copy-start | bytes 589828
  11.8 60.3 %copy-start.11 = (pred[8]{0:T(512)(128)(4,1)}, pred[8]{0:T(512)(128)(4,1)S(1)}, u32[]{:S(2)}) copy-start(pred[8]{0:T(512)(128)(4,1)S(1)} %broadcast_compare_fusion.1) | copy-start | bytes 28
  17.6 54.4 %copy-start.9 = (s32[8]{0:T(128)}, s32[8]{0:T(128)S(1)}, u32[]{:S(2)}) copy-start(s32[8]{0:T(128)S(1)} %select_reduce_fusion) | copy-start | bytes 100
  17.7 4.6 %copy-start.7 = (f32[2,16]{1,0:T(2,128)S(1)}, f32[2,16]{1,0:T(2,128)}, u32[]{:S(2)}) copy-start(f32[2,16]{1,0:T(2,128)} %param.12) | copy-start | bytes 388
  17.8 9.3 %copy-start.5 = (f32[4,4]{1,0:T(4,128)S(1)}, f32[4,4]{1,0:T(4,128)}, u32[]{:S(2)}) copy-start(f32[4,4]{1,0:T(4,128)} %param.14) | copy-start | bytes 196
  17.8 17.3 %copy-start.6 = (f32[16,2]{0,1:T(2,128)S(1)}, f32[16,2]{0,1:T(2,128)}, u32[]{:S(2)}) copy-start(f32[16,2]{0,1:T(2,128)} %param.13) | copy-start | bytes 388
  18.0 12.8 %collective-permute-start.5 = (f32[3,16,14,3]{3,1,2,0:T(8,128)S(1)}, f32[3,16,14,3]{3,1,2,0:T(8,128)S(1)}, u32[]{:S(2)}, u32[]{:S(2)}) collective-permute-start(f32[3,16,14,3]{3,1,2,0:T(8,128)S(1)} %get-tuple-element.20), channel_id=1, source_target_pairs={{0,1},{1,2},{2,3},{3,0},{4,5},{5,6},{6,7},{7,4},{8,9},{9,10},{10,1... | collective-permute-start | bytes 24200 | tf_op jit(solution)/shard_map/ppermute | solution.py:19
  19.6 15.5 %collective-permute-start.4 = (f32[3,16,14,3]{3,1,2,0:T(8,128)S(1)}, f32[3,16,14,3]{3,1,2,0:T(8,128)S(1)}, u32[]{:S(2)}, u32[]{:S(2)}) collective-permute-start(f32[3,16,14,3]{3,1,2,0:T(8,128)S(1)} %get-tuple-element.19), channel_id=1, source_target_pairs={{1,0},{2,1},{3,2},{0,3},{5,4},{6,5},{7,6},{4,7},{9,8},{10,9},{11,1... | collective-permute-start | bytes 24200 | tf_op jit(solution)/shard_map/ppermute | solution.py:21
  37.0 8.8 %collective-permute-start.7 = (f32[3,2,8,128]{3,1,2,0:T(2,128)S(1)}, f32[3,2,8,128]{3,1,2,0:T(2,128)S(1)}, u32[]{:S(2)}, u32[]{:S(2)}) collective-permute-start(f32[3,2,8,128]{3,1,2,0:T(2,128)S(1)} %get-tuple-element.42), channel_id=1, source_target_pairs={{0,16},{1,17},{2,18},{3,19},{4,20},{5,21},{6,22},{7,23},{8,24},{9,... | collective-permute-start | bytes 73736 | tf_op jit(solution)/shard_map/ppermute | solution.py:19
  40.7 5.7 %collective-permute-start.6 = (f32[3,2,8,128]{3,1,2,0:T(2,128)S(1)}, f32[3,2,8,128]{3,1,2,0:T(2,128)S(1)}, u32[]{:S(2)}, u32[]{:S(2)}) collective-permute-start(f32[3,2,8,128]{3,1,2,0:T(2,128)S(1)} %get-tuple-element.41), channel_id=1, source_target_pairs={{16,0},{17,1},{18,2},{19,3},{20,4},{21,5},{22,6},{23,7},{24,8},{25... | collective-permute-start | bytes 73736 | tf_op jit(solution)/shard_map/ppermute | solution.py:21
  44.0 7.8 %collective-permute-start.9 = (f32[3,16,3,128]{3,1,2,0:T(8,128)S(1)}, f32[3,16,3,128]{3,1,2,0:T(8,128)S(1)}, u32[]{:S(2)}, u32[]{:S(2)}) collective-permute-start(f32[3,16,3,128]{3,1,2,0:T(8,128)S(1)} %get-tuple-element.38), channel_id=1, source_target_pairs={{0,4},{4,8},{8,12},{12,0},{1,5},{5,9},{9,13},{13,1},{2,6},{6,10},{... | collective-permute-start | bytes 221192 | tf_op jit(solution)/shard_map/ppermute | solution.py:19
  44.1 7.8 %collective-permute-start.8 = (f32[3,16,3,128]{3,1,2,0:T(8,128)S(1)}, f32[3,16,3,128]{3,1,2,0:T(8,128)S(1)}, u32[]{:S(2)}, u32[]{:S(2)}) collective-permute-start(f32[3,16,3,128]{3,1,2,0:T(8,128)S(1)} %get-tuple-element.37), channel_id=1, source_target_pairs={{4,0},{8,4},{12,8},{0,12},{5,1},{9,5},{13,9},{1,13},{6,2},{10,6},{... | collective-permute-start | bytes 221192 | tf_op jit(solution)/shard_map/ppermute | solution.py:21
  52.1 12.8 %collective-permute-start.11 = (f32[3,16,14,3]{3,1,2,0:T(8,128)S(1)}, f32[3,16,14,3]{3,1,2,0:T(8,128)S(1)}, u32[]{:S(2)}, u32[]{:S(2)}) collective-permute-start(f32[3,16,14,3]{3,1,2,0:T(8,128)S(1)} %get-tuple-element.18), channel_id=1, source_target_pairs={{0,1},{1,2},{2,3},{3,0},{4,5},{5,6},{6,7},{7,4},{8,9},{9,10},{10,1... | collective-permute-start | bytes 24200 | tf_op jit(solution)/shard_map/ppermute | solution.py:19
  53.3 15.1 %collective-permute-start.10 = (f32[3,16,14,3]{3,1,2,0:T(8,128)S(1)}, f32[3,16,14,3]{3,1,2,0:T(8,128)S(1)}, u32[]{:S(2)}, u32[]{:S(2)}) collective-permute-start(f32[3,16,14,3]{3,1,2,0:T(8,128)S(1)} %get-tuple-element.17), channel_id=1, source_target_pairs={{1,0},{2,1},{3,2},{0,3},{5,4},{6,5},{7,6},{4,7},{9,8},{10,9},{11,1... | collective-permute-start | bytes 24200 | tf_op jit(solution)/shard_map/ppermute | solution.py:21
  73.1 10.8 %collective-permute-start.14 = (f32[6,16,3,128]{3,1,2,0:T(8,128)S(1)}, f32[6,16,3,128]{3,1,2,0:T(8,128)S(1)}, u32[]{:S(2)}, u32[]{:S(2)}) collective-permute-start(f32[6,16,3,128]{3,1,2,0:T(8,128)S(1)} %get-tuple-element.16), channel_id=1, source_target_pairs={{4,0},{8,4},{12,8},{0,12},{5,1},{9,5},{13,9},{1,13},{6,2},{10,6},{... | collective-permute-start | bytes 442376 | tf_op jit(solution)/shard_map/ppermute | solution.py:21
  73.3 10.6 %collective-permute-start.15 = (f32[6,16,3,128]{3,1,2,0:T(8,128)S(1)}, f32[6,16,3,128]{3,1,2,0:T(8,128)S(1)}, u32[]{:S(2)}, u32[]{:S(2)}) collective-permute-start(f32[6,16,3,128]{3,1,2,0:T(8,128)S(1)} %get-tuple-element.15), channel_id=1, source_target_pairs={{0,4},{4,8},{8,12},{12,0},{1,5},{5,9},{9,13},{13,1},{2,6},{6,10},{... | collective-permute-start | bytes 442376 | tf_op jit(solution)/shard_map/ppermute | solution.py:19
  79.0 18.2 %collective-permute-start.13 = (f32[3,2,8,128]{3,1,2,0:T(2,128)S(1)}, f32[3,2,8,128]{3,1,2,0:T(2,128)S(1)}, u32[]{:S(2)}, u32[]{:S(2)}) collective-permute-start(f32[3,2,8,128]{3,1,2,0:T(2,128)S(1)} %get-tuple-element.34), channel_id=1, source_target_pairs={{0,16},{1,17},{2,18},{3,19},{4,20},{5,21},{6,22},{7,23},{8,24},{9,... | collective-permute-start | bytes 73736 | tf_op jit(solution)/shard_map/ppermute | solution.py:19
  82.6 14.5 %collective-permute-start.12 = (f32[3,2,8,128]{3,1,2,0:T(2,128)S(1)}, f32[3,2,8,128]{3,1,2,0:T(2,128)S(1)}, u32[]{:S(2)}, u32[]{:S(2)}) collective-permute-start(f32[3,2,8,128]{3,1,2,0:T(2,128)S(1)} %get-tuple-element.33), channel_id=1, source_target_pairs={{16,0},{17,1},{18,2},{19,3},{20,4},{21,5},{22,6},{23,7},{24,8},{25... | collective-permute-start | bytes 73736 | tf_op jit(solution)/shard_map/ppermute | solution.py:21
  85.0 8.8 %collective-permute-start.17 = (f32[6,16,14,3]{2,1,3,0:T(8,128)S(1)}, f32[6,16,14,3]{2,1,3,0:T(8,128)S(1)}, u32[]{:S(2)}, u32[]{:S(2)}) collective-permute-start(f32[6,16,14,3]{2,1,3,0:T(8,128)S(1)} %copy.102), channel_id=1, source_target_pairs={{0,1},{1,2},{2,3},{3,0},{4,5},{5,6},{6,7},{7,4},{8,9},{9,10},{10,1... | collective-permute-start | bytes 48392 | tf_op jit(solution)/shard_map/ppermute | solution.py:19
  86.7 11.1 %copy-start.3 = (f32[16,8,128]{2,0,1:T(8,128)S(1)}, f32[16,8,128]{2,0,1:T(8,128)}, u32[]{:S(2)}) copy-start(f32[16,8,128]{2,0,1:T(8,128)} %copy.110) | copy-start | bytes 196612
  86.7 11.1 %copy-start.10 = (s32[8]{0:T(128)S(1)}, s32[8]{0:T(128)}, u32[]{:S(2)}) copy-start(s32[8]{0:T(128)} %copy-done.9) | copy-start | bytes 100
  86.7 11.1 %copy-start.12 = (pred[8]{0:T(512)(128)(4,1)S(1)}, pred[8]{0:T(512)(128)(4,1)}, u32[]{:S(2)}) copy-start(pred[8]{0:T(512)(128)(4,1)} %copy-done.11) | copy-start | bytes 28
  86.7 8.8 %collective-permute-start.16 = (f32[6,16,14,3]{2,1,3,0:T(8,128)S(1)}, f32[6,16,14,3]{2,1,3,0:T(8,128)}, u32[]{:S(2)}, u32[]{:S(2)}) collective-permute-start(f32[6,16,14,3]{2,1,3,0:T(8,128)S(1)} %copy.100), channel_id=1, source_target_pairs={{1,0},{2,1},{3,2},{0,3},{5,4},{6,5},{7,6},{4,7},{9,8},{10,9},{11,1... | collective-permute-start | bytes 48392 | tf_op jit(solution)/shard_map/ppermute | solution.py:21
  97.2 0.6 copy-start.14
  97.2 0.6 copy-start.15
  100.0 6.4 %copy-start.8 = (f32[2,16]{1,0:T(2,128)S(1)}, f32[2,16]{1,0:T(2,128)}, u32[]{:S(2)}) copy-start(f32[2,16]{1,0:T(2,128)} %param.12) | copy-start | bytes 388
  105.8 7.4 %collective-permute-start.20 = (f32[6,16,3,128]{3,1,2,0:T(8,128)S(1)}, f32[6,16,3,128]{3,1,2,0:T(8,128)S(1)}, u32[]{:S(2)}, u32[]{:S(2)}) collective-permute-start(f32[6,16,3,128]{3,1,2,0:T(8,128)S(1)} %get-tuple-element.12), channel_id=1, source_target_pairs={{4,0},{8,4},{12,8},{0,12},{5,1},{9,5},{13,9},{1,13},{6,2},{10,6},{... | collective-permute-start | bytes 442376 | tf_op jit(solution)/shard_map/ppermute | solution.py:21
  105.8 7.4 %collective-permute-start.21 = (f32[6,16,3,128]{3,1,2,0:T(8,128)S(1)}, f32[6,16,3,128]{3,1,2,0:T(8,128)S(1)}, u32[]{:S(2)}, u32[]{:S(2)}) collective-permute-start(f32[6,16,3,128]{3,1,2,0:T(8,128)S(1)} %get-tuple-element.11), channel_id=1, source_target_pairs={{0,4},{4,8},{8,12},{12,0},{1,5},{5,9},{9,13},{13,1},{2,6},{6,10},{... | collective-permute-start | bytes 442376 | tf_op jit(solution)/shard_map/ppermute | solution.py:19
  106.7 10.1 %copy-start.2 = (f32[3,16,8,128]{3,1,2,0:T(8,128)}, f32[3,16,8,128]{3,1,2,0:T(8,128)S(1)}, u32[]{:S(2)}) copy-start(f32[3,16,8,128]{3,1,2,0:T(8,128)S(1)} %fusion.5) | copy-start | bytes 589828
  107.4 19.8 %collective-permute-start.19 = (f32[3,2,8,128]{3,1,2,0:T(2,128)}, f32[3,2,8,128]{3,1,2,0:T(2,128)}, u32[]{:S(2)}, u32[]{:S(2)}) collective-permute-start(f32[3,2,8,128]{3,1,2,0:T(2,128)} %get-tuple-element.27), channel_id=1, source_target_pairs={{0,16},{1,17},{2,18},{3,19},{4,20},{5,21},{6,22},{7,23},{8,24},{9,... | collective-permute-start | bytes 73736 | tf_op jit(solution)/shard_map/ppermute | solution.py:19
  111.9 15.3 %collective-permute-start.18 = (f32[3,2,8,128]{3,1,2,0:T(2,128)}, f32[3,2,8,128]{3,1,2,0:T(2,128)}, u32[]{:S(2)}, u32[]{:S(2)}) collective-permute-start(f32[3,2,8,128]{3,1,2,0:T(2,128)} %get-tuple-element.26), channel_id=1, source_target_pairs={{16,0},{17,1},{18,2},{19,3},{20,4},{21,5},{22,6},{23,7},{24,8},{25... | collective-permute-start | bytes 73736 | tf_op jit(solution)/shard_map/ppermute | solution.py:21
  115.0 8.8 %collective-permute-start.23 = (f32[6,16,14,3]{2,1,3,0:T(8,128)}, f32[6,16,14,3]{2,1,3,0:T(8,128)S(1)}, u32[]{:S(2)}, u32[]{:S(2)}) collective-permute-start(f32[6,16,14,3]{2,1,3,0:T(8,128)} %copy.114), channel_id=1, source_target_pairs={{0,1},{1,2},{2,3},{3,0},{4,5},{5,6},{6,7},{7,4},{8,9},{9,10},{10,1... | collective-permute-start | bytes 48392 | tf_op jit(solution)/shard_map/ppermute | solution.py:19
  116.8 8.7 %collective-permute-start.22 = (f32[6,16,14,3]{2,1,3,0:T(8,128)S(1)}, f32[6,16,14,3]{2,1,3,0:T(8,128)}, u32[]{:S(2)}, u32[]{:S(2)}) collective-permute-start(f32[6,16,14,3]{2,1,3,0:T(8,128)S(1)} %copy.112), channel_id=1, source_target_pairs={{1,0},{2,1},{3,2},{0,3},{5,4},{6,5},{7,6},{4,7},{9,8},{10,9},{11,1... | collective-permute-start | bytes 48392 | tf_op jit(solution)/shard_map/ppermute | solution.py:21
where the time goes:
time: 130 us
  starting transfers between devices  42.3 us (33%)
  waiting for transfers between devices  29.4 us (23%)
  blocking collectives  23.5 us (18%)
  local copies, waits for them, and re-layouts  18.1 us (14%)
  matrix products  9.75 us (8%)
  other arithmetic  5.91 us (5%)
    ppermute x12, starting transfers between devices, extended(): lax.ppermute(tail, axis, [(i, (i + 1) % count) for i in range(ends)])  22.3 us
    ppermute x12, starting transfers between devices, extended(): lax.ppermute(head, axis, [((i + 1) % count, i) for i in range(ends)])  20 us
    ppermute x12, waiting for transfers between devices, extended(): lax.ppermute(tail, axis, [(i, (i + 1) % count) for i in range(ends)])  19 us
    all_gather x4, blocking collectives, interface_sum(): lax.all_gather(edge_values, 'gx', axis=0, tiled=True)  18.4 us
    ppermute x12, waiting for transfers between devices, extended(): lax.ppermute(head, axis, [((i + 1) % count, i) for i in range(ends)])  10.4 us
    all_gather x1, blocking collectives, local(): every_inv = lax.all_gather(inverse_here, 'gx', axis=0, tiled=True)  5.17 us
    ppermute x2, local copies, waits for them, and re-layouts, extended(): lax.ppermute(head, axis, [((i + 1) % count, i) for i in range(ends)])  3.3 us
    slice x12, local copies, waits for them, and re-layouts, extended(): head = lax.slice_in_dim(cells, 0, width, axis=dim)  3.04 us
  transfers between devices with their start and end apart: 24, of which 9 were waited for; matrix products, arithmetic and copies ran while one was open for 15% of the time, Pallas kernels for 0%

commit v1 on v0

--- a/solution.py
+++ b/solution.py
@@ -6,6 +6,18 @@
 WIN = 8
 time_step = 0.15
 high = lax.Precision.HIGHEST
+
+
+def summed_around(shard, axis, dim, contribution):
+    size, index = (lax.axis_size(axis), lax.axis_index(axis))
+    backward = [(i, (i - 1) % size) for i in range(size)]
+    extent = shard.shape[dim]
+    current = shard
+    so_far = contribution(current, index * extent)
+    for step in range(1, size):
+        current = lax.ppermute(current, axis, backward)
+        so_far = so_far + contribution(current, (index + step) % size * extent)
+    return so_far
 
 
 def extended(cells, sides, width, closed):
@@ -64,11 +76,16 @@
 
 
 def interface_sum(edge_values, weight_cols):
-    return jnp.einsum(
-        "ma,mcyz->acyz",
-        weight_cols,
-        lax.all_gather(edge_values, "gx", axis=0, tiled=True),
-        precision=high,
+    return summed_around(
+        edge_values,
+        "gx",
+        0,
+        lambda part, at: jnp.einsum(
+            "ma,mcyz->acyz",
+            lax.dynamic_slice_in_dim(weight_cols, at, part.shape[0], axis=0),
+            part,
+            precision=high,
+        ),
     )
 
 

time: 130 us -> 125 us (0.962)
  blocking collectives: 23.5 us -> 5.17 us
  starting transfers between devices: 42.3 us -> 50.8 us
  waiting for transfers between devices: 29.4 us -> 31.9 us
  matrix products: 9.75 us -> 11.2 us
    all_gather x4 -> x0, blocking collectives: 18.4 us -> none  [interface_sum(): lax.all_gather(edge_values, 'gx', axis=0, tiled=True)]
    ppermute x0 -> x4, starting transfers between devices: none -> 8.47 us  [summed_around(): current = lax.ppermute(current, axis, backward)]
    ppermute x0 -> x4, waiting for transfers between devices: none -> 5.71 us  [summed_around(): current = lax.ppermute(current, axis, backward)]
    ppermute x12, waiting for transfers between devices: 19 us -> 17.1 us  [extended(): lax.ppermute(tail, axis, [(i, (i + 1) % count) for i in range(ends)])]
    dot_general x4 -> x8, matrix products: 1.14 us -> 2.56 us  [interface_sum(): jnp.einsum('ma,mcyz->acyz', lax.dynamic_slice_in_dim(weight_cols, at, par...]
    ppermute x12, waiting for transfers between devices: 10.4 us -> 9.05 us  [extended(): lax.ppermute(head, axis, [((i + 1) % count, i) for i in range(ends)])]
  transfers between devices with their start and end apart: 24 -> 28, of which waited for: 9 -> 13; matrix products, arithmetic and copies ran while one was open for 15% -> 17% of each run, Pallas kernels for 0% -> 0%
where the time goes in v1:
time: 125 us; the launch traced here: 124 us
  starting transfers between devices  50.8 us (41%)
  waiting for transfers between devices  31.9 us (26%)
  local copies, waits for them, and re-layouts  18.1 us (14%)
  matrix products  11.2 us (9%)
  other arithmetic  5.95 us (5%)
  blocking collectives  5.17 us (4%)
    ppermute x12, starting transfers between devices, extended(): lax.ppermute(tail, axis, [(i, (i + 1) % count) for i in range(ends)])  22 us
    ppermute x12, starting transfers between devices, extended(): lax.ppermute(head, axis, [((i + 1) % count, i) for i in range(ends)])  20.3 us
    ppermute x12, waiting for transfers between devices, extended(): lax.ppermute(tail, axis, [(i, (i + 1) % count) for i in range(ends)])  17.1 us
    ppermute x12, waiting for transfers between devices, extended(): lax.ppermute(head, axis, [((i + 1) % count, i) for i in range(ends)])  9.05 us
    ppermute x4, starting transfers between devices, summed_around(): current = lax.ppermute(current, axis, backward)  8.47 us
    ppermute x4, waiting for transfers between devices, summed_around(): current = lax.ppermute(current, axis, backward)  5.71 us
    all_gather x1, blocking collectives, local(): every_inv = lax.all_gather(inverse_here, 'gx', axis=0, tiled=True)  5.17 us
    ppermute x2, local copies, waits for them, and re-layouts, extended(): lax.ppermute(head, axis, [((i + 1) % count, i) for i in range(ends)])  3.3 us
  transfers between devices with their start and end apart: 28, of which 13 were waited for; matrix products, arithmetic and copies ran while one was open for 17% of the time, Pallas kernels for 0%

profile of v1, /device:TPU:0, one launch (start us, length us, event | category | flops | bytes accessed | tf_op | source)
XLA Modules:
  0.0 123.9 jit_solution(15473751895877319537)
XLA Ops:
  0.0 1.0 copy.82
  1.6 2.0 %collective-permute-start.3 = (f32[3,16,3,128]{3,1,2,0:T(8,128)S(1)}, f32[3,16,3,128]{3,1,2,0:T(8,128)S(1)}, u32[]{:S(2)}, u32[]{:S(2)}) collective-permute-start(f32[3,16,3,128]{3,1,2,0:T(8,128)S(1)} %get-tuple-element.51), channel_id=1, source_target_pairs={{4,0},{8,4},{12,8},{0,12},{5,1},{9,5},{13,9},{1,13},{6,2},{10,6},{... | collective-permute-start | bytes 221192 | tf_op jit(solution)/shard_map/ppermute | solution.py:33
  3.6 4.2 %collective-permute-start.1 = (f32[3,2,8,128]{3,1,2,0:T(2,128)S(1)}, f32[3,2,8,128]{3,1,2,0:T(2,128)S(1)}, u32[]{:S(2)}, u32[]{:S(2)}) collective-permute-start(f32[3,2,8,128]{3,1,2,0:T(2,128)S(1)} %get-tuple-element.44), channel_id=1, source_target_pairs={{0,16},{1,17},{2,18},{3,19},{4,20},{5,21},{6,22},{7,23},{8,24},{9,... | collective-permute-start | bytes 73736 | tf_op jit(solution)/shard_map/ppermute | solution.py:31
  7.8 1.3 %collective-permute-start = (f32[3,2,8,128]{3,1,2,0:T(2,128)S(1)}, f32[3,2,8,128]{3,1,2,0:T(2,128)S(1)}, u32[]{:S(2)}, u32[]{:S(2)}) collective-permute-start(f32[3,2,8,128]{3,1,2,0:T(2,128)S(1)} %get-tuple-element.43), channel_id=1, source_target_pairs={{16,0},{17,1},{18,2},{19,3},{20,4},{21,5},{22,6},{23,7},{24,8},{25... | collective-permute-start | bytes 73736 | tf_op jit(solution)/shard_map/ppermute | solution.py:33
  9.1 1.0 slice_convert_fusion
  12.1 5.2 %all-gather = f32[8,1,1,16,16]{4,3,2,1,0:T(8,128)S(1)} all-gather(f32[4,1,1,16,16]{4,3,2,1,0:T(8,128)S(1)} %copy-done.4), channel_id=2, replica_groups=mesh['gx'=2,'gy'=4,'gz'=4] {'gx'}, dimensions={0}, use_global_device_ids=true | all-gather | bytes 12288 | tf_op jit(solution)/shard_map/all_gather | solution.py:156
  18.0 1.6 %collective-permute-start.6 = (f32[3,16,14,3]{3,1,2,0:T(8,128)S(1)}, f32[3,16,14,3]{3,1,2,0:T(8,128)S(1)}, u32[]{:S(2)}, u32[]{:S(2)}) collective-permute-start(f32[3,16,14,3]{3,1,2,0:T(8,128)S(1)} %get-tuple-element.20), channel_id=1, source_target_pairs={{0,1},{1,2},{2,3},{3,0},{4,5},{5,6},{6,7},{7,4},{8,9},{9,10},{10,1... | collective-permute-start | bytes 24200 | tf_op jit(solution)/shard_map/ppermute | solution.py:31
  19.6 2.2 %collective-permute-start.5 = (f32[3,16,14,3]{3,1,2,0:T(8,128)S(1)}, f32[3,16,14,3]{3,1,2,0:T(8,128)S(1)}, u32[]{:S(2)}, u32[]{:S(2)}) collective-permute-start(f32[3,16,14,3]{3,1,2,0:T(8,128)S(1)} %get-tuple-element.19), channel_id=1, source_target_pairs={{1,0},{2,1},{3,2},{0,3},{5,4},{6,5},{7,6},{4,7},{9,8},{10,9},{11,1... | collective-permute-start | bytes 24200 | tf_op jit(solution)/shard_map/ppermute | solution.py:33
  22.6 2.1 %collective-permute-start.2 = (f32[2,3,8,128]{3,0,2,1:T(2,128)S(1)}, f32[2,3,8,128]{3,0,2,1:T(2,128)S(1)}, u32[]{:S(2)}, u32[]{:S(2)}) collective-permute-start(f32[2,3,8,128]{3,0,2,1:T(2,128)S(1)} %convolution_bitcast_fusion.6), channel_id=1, source_target_pairs={{0,16},{16,0},{1,17},{17,1},{2,18},{18,2},{3,19},{19,3},{4,20},{20... | collective-permute-start | bytes 73736 | tf_op jit(solution)/shard_map/ppermute | solution.py:18
  25.0 1.5 %collective-permute-done.2 = f32[2,3,8,128]{3,0,2,1:T(2,128)S(1)} collective-permute-done((f32[2,3,8,128]{3,0,2,1:T(2,128)S(1)}, f32[2,3,8,128]{3,0,2,1:T(2,128)S(1)}, u32[]{:S(2)}, u32[]{:S(2)}) %collective-permute-start.2) | collective-permute-done | bytes 24608 | tf_op jit(solution)/shard_map/ppermute | solution.py:18
  26.8 4.0 %collective-permute-done.6 = f32[3,16,14,3]{3,1,2,0:T(8,128)S(1)} collective-permute-done((f32[3,16,14,3]{3,1,2,0:T(8,128)S(1)}, f32[3,16,14,3]{3,1,2,0:T(8,128)S(1)}, u32[]{:S(2)}, u32[]{:S(2)}) %collective-permute-start.6) | collective-permute-done | bytes 8096 | tf_op jit(solution)/shard_map/ppermute | solution.py:31
  30.8 4.3 %collective-permute-done.5 = f32[3,16,14,3]{3,1,2,0:T(8,128)S(1)} collective-permute-done((f32[3,16,14,3]{3,1,2,0:T(8,128)S(1)}, f32[3,16,14,3]{3,1,2,0:T(8,128)S(1)}, u32[]{:S(2)}, u32[]{:S(2)}) %collective-permute-start.5) | collective-permute-done | bytes 8096 | tf_op jit(solution)/shard_map/ppermute | solution.py:33
  35.1 0.8 fusion.90
  36.2 0.8 reshape.79
  37.1 3.7 %collective-permute-start.8 = (f32[3,2,8,128]{3,1,2,0:T(2,128)S(1)}, f32[3,2,8,128]{3,1,2,0:T(2,128)S(1)}, u32[]{:S(2)}, u32[]{:S(2)}) collective-permute-start(f32[3,2,8,128]{3,1,2,0:T(2,128)S(1)} %get-tuple-element.42), channel_id=1, source_target_pairs={{0,16},{1,17},{2,18},{3,19},{4,20},{5,21},{6,22},{7,23},{8,24},{9,... | collective-permute-start | bytes 73736 | tf_op jit(solution)/shard_map/ppermute | solution.py:31
  40.7 1.3 %collective-permute-start.7 = (f32[3,2,8,128]{3,1,2,0:T(2,128)S(1)}, f32[3,2,8,128]{3,1,2,0:T(2,128)S(1)}, u32[]{:S(2)}, u32[]{:S(2)}) collective-permute-start(f32[3,2,8,128]{3,1,2,0:T(2,128)S(1)} %get-tuple-element.41), channel_id=1, source_target_pairs={{16,0},{17,1},{18,2},{19,3},{20,4},{21,5},{22,6},{23,7},{24,8},{25... | collective-permute-start | bytes 73736 | tf_op jit(solution)/shard_map/ppermute | solution.py:33
  43.3 0.8 div.55
  44.1 1.7 %collective-permute-start.10 = (f32[3,16,3,128]{3,1,2,0:T(8,128)S(1)}, f32[3,16,3,128]{3,1,2,0:T(8,128)S(1)}, u32[]{:S(2)}, u32[]{:S(2)}) collective-permute-start(f32[3,16,3,128]{3,1,2,0:T(8,128)S(1)} %get-tuple-element.37), channel_id=1, source_target_pairs={{4,0},{8,4},{12,8},{0,12},{5,1},{9,5},{13,9},{1,13},{6,2},{10,6},{... | collective-permute-start | bytes 221192 | tf_op jit(solution)/shard_map/ppermute | solution.py:33
  47.1 2.1 %collective-permute-start.9 = (f32[2,3,8,128]{3,0,2,1:T(2,128)S(1)}, f32[2,3,8,128]{3,0,2,1:T(2,128)S(1)}, u32[]{:S(2)}, u32[]{:S(2)}) collective-permute-start(f32[2,3,8,128]{3,0,2,1:T(2,128)S(1)} %convolution_bitcast_fusion.5), channel_id=1, source_target_pairs={{0,16},{16,0},{1,17},{17,1},{2,18},{18,2},{3,19},{19,3},{4,20},{20... | collective-permute-start | bytes 73736 | tf_op jit(solution)/shard_map/ppermute | solution.py:18
  49.5 1.5 %collective-permute-done.9 = f32[2,3,8,128]{3,0,2,1:T(2,128)S(1)} collective-permute-done((f32[2,3,8,128]{3,0,2,1:T(2,128)S(1)}, f32[2,3,8,128]{3,0,2,1:T(2,128)S(1)}, u32[]{:S(2)}, u32[]{:S(2)}) %collective-permute-start.9) | collective-permute-done | bytes 24608 | tf_op jit(solution)/shard_map/ppermute | solution.py:18
  51.6 1.2 collective-permute-start.13
  52.8 2.7 %collective-permute-start.12 = (f32[3,16,14,3]{3,1,2,0:T(8,128)S(1)}, f32[3,16,14,3]{3,1,2,0:T(8,128)S(1)}, u32[]{:S(2)}, u32[]{:S(2)}) collective-permute-start(f32[3,16,14,3]{3,1,2,0:T(8,128)S(1)} %get-tuple-element.17), channel_id=1, source_target_pairs={{1,0},{2,1},{3,2},{0,3},{5,4},{6,5},{7,6},{4,7},{9,8},{10,9},{11,1... | collective-permute-start | bytes 24200 | tf_op jit(solution)/shard_map/ppermute | solution.py:33
  55.8 8.5 %collective-permute-done.13 = f32[3,16,14,3]{3,1,2,0:T(8,128)S(1)} collective-permute-done((f32[3,16,14,3]{3,1,2,0:T(8,128)S(1)}, f32[3,16,14,3]{3,1,2,0:T(8,128)S(1)}, u32[]{:S(2)}, u32[]{:S(2)}) %collective-permute-start.13) | collective-permute-done | bytes 8096 | tf_op jit(solution)/shard_map/ppermute | solution.py:31
  64.4 3.5 %collective-permute-done.12 = f32[3,16,14,3]{3,1,2,0:T(8,128)S(1)} collective-permute-done((f32[3,16,14,3]{3,1,2,0:T(8,128)S(1)}, f32[3,16,14,3]{3,1,2,0:T(8,128)S(1)}, u32[]{:S(2)}, u32[]{:S(2)}) %collective-permute-start.12) | collective-permute-done | bytes 8096 | tf_op jit(solution)/shard_map/ppermute | solution.py:33
  67.9 0.8 fusion.102
  68.7 0.8 reshape.77
  70.8 0.8 div.50
  72.9 1.8 %collective-permute-start.14 = (f32[2,3,8,128]{3,0,2,1:T(2,128)S(1)}, f32[2,3,8,128]{3,0,2,1:T(2,128)S(1)}, u32[]{:S(2)}, u32[]{:S(2)}) collective-permute-start(f32[2,3,8,128]{3,0,2,1:T(2,128)S(1)} %convolution_bitcast_fusion.4), channel_id=1, source_target_pairs={{0,16},{16,0},{1,17},{17,1},{2,18},{18,2},{3,19},{19,3},{4,20},{20... | collective-permute-start | bytes 73736 | tf_op jit(solution)/shard_map/ppermute | solution.py:18
  75.3 1.5 %collective-permute-done.14 = f32[2,3,8,128]{3,0,2,1:T(2,128)S(1)} collective-permute-done((f32[2,3,8,128]{3,0,2,1:T(2,128)S(1)}, f32[2,3,8,128]{3,0,2,1:T(2,128)S(1)}, u32[]{:S(2)}, u32[]{:S(2)}) %collective-permute-start.14) | collective-permute-done | bytes 24608 | tf_op jit(solution)/shard_map/ppermute | solution.py:18
  77.6 3.7 %collective-permute-start.16 = (f32[3,2,8,128]{3,1,2,0:T(2,128)S(1)}, f32[3,2,8,128]{3,1,2,0:T(2,128)S(1)}, u32[]{:S(2)}, u32[]{:S(2)}) collective-permute-start(f32[3,2,8,128]{3,1,2,0:T(2,128)S(1)} %get-tuple-element.34), channel_id=1, source_target_pairs={{0,16},{1,17},{2,18},{3,19},{4,20},{5,21},{6,22},{7,23},{8,24},{9,... | collective-permute-start | bytes 73736 | tf_op jit(solution)/shard_map/ppermute | solution.py:31
  81.2 1.5 %collective-permute-start.15 = (f32[3,2,8,128]{3,1,2,0:T(2,128)S(1)}, f32[3,2,8,128]{3,1,2,0:T(2,128)S(1)}, u32[]{:S(2)}, u32[]{:S(2)}) collective-permute-start(f32[3,2,8,128]{3,1,2,0:T(2,128)S(1)} %get-tuple-element.33), channel_id=1, source_target_pairs={{16,0},{17,1},{18,2},{19,3},{20,4},{21,5},{22,6},{23,7},{24,8},{25... | collective-permute-start | bytes 73736 | tf_op jit(solution)/shard_map/ppermute | solution.py:33
  83.8 0.8 collective-permute-start.20
  85.3 3.1 %collective-permute-start.19 = (f32[6,16,14,3]{2,1,3,0:T(8,128)S(1)}, f32[6,16,14,3]{2,1,3,0:T(8,128)}, u32[]{:S(2)}, u32[]{:S(2)}) collective-permute-start(f32[6,16,14,3]{2,1,3,0:T(8,128)S(1)} %copy.95), channel_id=1, source_target_pairs={{1,0},{2,1},{3,2},{0,3},{5,4},{6,5},{7,6},{4,7},{9,8},{10,9},{11,1... | collective-permute-start | bytes 48392 | tf_op jit(solution)/shard_map/ppermute | solution.py:33
  88.4 1.1 pad_maximum_fusion.2
  89.5 1.9 %collective-permute-done.20 = f32[6,16,14,3]{2,1,3,0:T(8,128)S(1)} collective-permute-done((f32[6,16,14,3]{2,1,3,0:T(8,128)S(1)}, f32[6,16,14,3]{2,1,3,0:T(8,128)S(1)}, u32[]{:S(2)}, u32[]{:S(2)}) %collective-permute-start.20) | collective-permute-done | bytes 16160 | tf_op jit(solution)/shard_map/ppermute | solution.py:31
  91.4 0.8 copy.98
  92.5 1.7 %copy.96 = f32[6,16,14,3]{3,1,2,0:T(8,128)S(1)} copy(f32[6,16,14,3]{2,1,3,0:T(8,128)} %collective-permute-done.19) | data formatting | bytes 32256 | tf_op jit(solution)/shard_map/ppermute | solution.py:33
  94.8 2.1 %broadcast_multiply_fusion.1 = (f32[3,16,8,128]{3,1,2,0:T(8,128)S(1)}, f32[3,16,8,128]{3,1,2,0:T(8,128)S(1)}, f32[3,16,8,128]{3,1,2,0:T(8,128)S(1)}) fusion(f32[16,8,128]{2,0,1:T(8,128)S(1)} %copy-done.3, f32[16,8,128]{2,0,1:T(8,128)} %copy.105, s32[8]{0:T(128)S(1)} %copy-done.10, pred[8]{0:T(512)(128)(4,1)S(1)} %copy-done.12, ...), kind=kOutput, calls=%fused_computation.213 | convolution fusion | flops 7471360 | bytes 3161640 | tf_op jit(solution)/shard_map/sx,scyz->cxyz/dot_general | solution.py:154
  97.9 2.4 %collective-permute-start.21 = (f32[2,3,8,128]{3,0,2,1:T(2,128)S(1)}, f32[2,3,8,128]{3,0,2,1:T(2,128)S(1)}, u32[]{:S(2)}, u32[]{:S(2)}) collective-permute-start(f32[2,3,8,128]{3,0,2,1:T(2,128)S(1)} %convolution_bitcast_fusion.3), channel_id=1, source_target_pairs={{0,16},{16,0},{1,17},{17,1},{2,18},{18,2},{3,19},{19,3},{4,20},{20... | collective-permute-start | bytes 73736 | tf_op jit(solution)/shard_map/ppermute | solution.py:18
  100.9 1.2 collective-permute-done.21
  103.5 4.5 %collective-permute-start.23 = (f32[3,2,8,128]{3,1,2,0:T(2,128)}, f32[3,2,8,128]{3,1,2,0:T(2,128)}, u32[]{:S(2)}, u32[]{:S(2)}) collective-permute-start(f32[3,2,8,128]{3,1,2,0:T(2,128)} %get-tuple-element.27), channel_id=1, source_target_pairs={{0,16},{1,17},{2,18},{3,19},{4,20},{5,21},{6,22},{7,23},{8,24},{9,... | collective-permute-start | bytes 73736 | tf_op jit(solution)/shard_map/ppermute | solution.py:31
  108.1 1.3 %collective-permute-start.22 = (f32[3,2,8,128]{3,1,2,0:T(2,128)}, f32[3,2,8,128]{3,1,2,0:T(2,128)}, u32[]{:S(2)}, u32[]{:S(2)}) collective-permute-start(f32[3,2,8,128]{3,1,2,0:T(2,128)} %get-tuple-element.26), channel_id=1, source_target_pairs={{16,0},{17,1},{18,2},{19,3},{20,4},{21,5},{22,6},{23,7},{24,8},{25... | collective-permute-start | bytes 73736 | tf_op jit(solution)/shard_map/ppermute | solution.py:33
  109.7 1.4 %copy.108 = f32[6,16,14,3]{2,1,3,0:T(8,128)} copy(f32[6,16,14,3]{3,1,2,0:T(8,128)S(1)} %get-tuple-element.6) | data formatting | bytes 32256 | tf_op jit(solution)/shard_map/slice | solution.py:28
  111.1 0.8 collective-permute-start.27
  112.7 3.0 %collective-permute-start.26 = (f32[6,16,14,3]{2,1,3,0:T(8,128)S(1)}, f32[6,16,14,3]{2,1,3,0:T(8,128)}, u32[]{:S(2)}, u32[]{:S(2)}) collective-permute-start(f32[6,16,14,3]{2,1,3,0:T(8,128)S(1)} %copy.106), channel_id=1, source_target_pairs={{1,0},{2,1},{3,2},{0,3},{5,4},{6,5},{7,6},{4,7},{9,8},{10,9},{11,1... | collective-permute-start | bytes 48392 | tf_op jit(solution)/shard_map/ppermute | solution.py:33
  115.8 2.6 %collective-permute-done.27 = f32[6,16,14,3]{2,1,3,0:T(8,128)S(1)} collective-permute-done((f32[6,16,14,3]{2,1,3,0:T(8,128)}, f32[6,16,14,3]{2,1,3,0:T(8,128)S(1)}, u32[]{:S(2)}, u32[]{:S(2)}) %collective-permute-start.27) | collective-permute-done | bytes 16160 | tf_op jit(solution)/shard_map/ppermute | solution.py:31
  119.5 1.7 %copy.107 = f32[6,16,14,3]{3,1,2,0:T(8,128)S(1)} copy(f32[6,16,14,3]{2,1,3,0:T(8,128)} %collective-permute-done.26) | data formatting | bytes 32256 | tf_op jit(solution)/shard_map/ppermute | solution.py:33
  121.2 2.0 %fusion.30 = f32[3,16,8,128]{3,1,2,0:T(8,128)S(1)} fusion(f32[3,16,8,128]{3,1,2,0:T(8,128)S(1)} %get-tuple-element.62, f32[3,2,8,128]{3,1,2,0:T(2,128)} %collective-permute-done.23, f32[3,16,8,128]{3,1,2,0:T(8,128)} %copy-done.2, f32[3,2,8,128]{3,1,2,0:T(2,128)} %collective-permute-done.22, f32[6,16,14,3]{3,1,2,0:T(8,128)S(1)} %copy.109, ...), kind=kLoop, calls=%fused_computation.77 | loop fusion | flops 2654208 | bytes 2735616 | tf_op jit(solution)/shard_map/add | solution.py:181
  (136 shorter events, 20.8 us)
Async XLA Ops:
  0.0 22.0 %copy-start = (f32[16,16]{1,0:T(8,128)S(1)}, f32[16,16]{1,0:T(8,128)}, u32[]{:S(2)}) copy-start(f32[16,16]{1,0:T(8,128)} %param.11) | copy-start | bytes 3076
  0.0 11.4 %copy-start.13 = (s32[8]{0:T(128)S(1)}, s32[8]{0:T(128)}, u32[]{:S(2)}) copy-start(s32[8]{0:T(128)} %param.15) | copy-start | bytes 100
  1.0 10.9 %copy-start.16 = (s32[8]{0:T(128)S(1)}, s32[8]{0:T(128)}, u32[]{:S(2)}) copy-start(s32[8]{0:T(128)} %param.16) | copy-start | bytes 100
  1.0 11.1 %copy-start.4 = (f32[4,1,1,16,16]{4,3,2,1,0:T(8,128)S(1)}, f32[4,1,1,16,16]{4,3,2,1,0:T(8,128)}, u32[]{:S(2)}) copy-start(f32[4,1,1,16,16]{4,3,2,1,0:T(8,128)} %param.17) | copy-start | bytes 12292
  1.0 16.6 %collective-permute-start.4 = (f32[3,16,3,128]{3,1,2,0:T(8,128)S(1)}, f32[3,16,3,128]{3,1,2,0:T(8,128)S(1)}, u32[]{:S(2)}, u32[]{:S(2)}) collective-permute-start(f32[3,16,3,128]{3,1,2,0:T(8,128)S(1)} %get-tuple-element.52), channel_id=1, source_target_pairs={{0,4},{4,8},{8,12},{12,0},{1,5},{5,9},{9,13},{13,1},{2,6},{6,10},{... | collective-permute-start | bytes 221192 | tf_op jit(solution)/shard_map/ppermute | solution.py:31
  1.6 16.2 %collective-permute-start.3 = (f32[3,16,3,128]{3,1,2,0:T(8,128)S(1)}, f32[3,16,3,128]{3,1,2,0:T(8,128)S(1)}, u32[]{:S(2)}, u32[]{:S(2)}) collective-permute-start(f32[3,16,3,128]{3,1,2,0:T(8,128)S(1)} %get-tuple-element.51), channel_id=1, source_target_pairs={{4,0},{8,4},{12,8},{0,12},{5,1},{9,5},{13,9},{1,13},{6,2},{10,6},{... | collective-permute-start | bytes 221192 | tf_op jit(solution)/shard_map/ppermute | solution.py:33
  3.6 18.3 %collective-permute-start.1 = (f32[3,2,8,128]{3,1,2,0:T(2,128)S(1)}, f32[3,2,8,128]{3,1,2,0:T(2,128)S(1)}, u32[]{:S(2)}, u32[]{:S(2)}) collective-permute-start(f32[3,2,8,128]{3,1,2,0:T(2,128)S(1)} %get-tuple-element.44), channel_id=1, source_target_pairs={{0,16},{1,17},{2,18},{3,19},{4,20},{5,21},{6,22},{7,23},{8,24},{9,... | collective-permute-start | bytes 73736 | tf_op jit(solution)/shard_map/ppermute | solution.py:31
  7.8 14.1 %collective-permute-start = (f32[3,2,8,128]{3,1,2,0:T(2,128)S(1)}, f32[3,2,8,128]{3,1,2,0:T(2,128)S(1)}, u32[]{:S(2)}, u32[]{:S(2)}) collective-permute-start(f32[3,2,8,128]{3,1,2,0:T(2,128)S(1)} %get-tuple-element.43), channel_id=1, source_target_pairs={{16,0},{17,1},{18,2},{19,3},{20,4},{21,5},{22,6},{23,7},{24,8},{25... | collective-permute-start | bytes 73736 | tf_op jit(solution)/shard_map/ppermute | solution.py:33
  10.0 7.7 %copy-start.1 = (f32[3,16,8,128]{3,2,1,0:T(8,128)S(1)}, f32[3,16,8,128]{3,2,1,0:T(8,128)}, u32[]{:S(2)}) copy-start(f32[3,16,8,128]{3,2,1,0:T(8,128)} %param.9) | copy-start | bytes 589828
  11.8 59.8 %copy-start.11 = (pred[8]{0:T(512)(128)(4,1)}, pred[8]{0:T(512)(128)(4,1)S(1)}, u32[]{:S(2)}) copy-start(pred[8]{0:T(512)(128)(4,1)S(1)} %broadcast_compare_fusion.1) | copy-start | bytes 28
  17.7 53.9 %copy-start.9 = (s32[8]{0:T(128)}, s32[8]{0:T(128)S(1)}, u32[]{:S(2)}) copy-start(s32[8]{0:T(128)S(1)} %select_reduce_fusion) | copy-start | bytes 100
  17.8 4.6 %copy-start.6 = (f32[2,16]{1,0:T(2,128)S(1)}, f32[2,16]{1,0:T(2,128)}, u32[]{:S(2)}) copy-start(f32[2,16]{1,0:T(2,128)} %param.12) | copy-start | bytes 388
  17.8 6.9 %copy-start.7 = (f32[4,4]{1,0:T(4,128)S(1)}, f32[4,4]{1,0:T(4,128)}, u32[]{:S(2)}) copy-start(f32[4,4]{1,0:T(4,128)} %param.14) | copy-start | bytes 196
  17.8 17.3 %copy-start.5 = (f32[16,2]{0,1:T(2,128)S(1)}, f32[16,2]{0,1:T(2,128)}, u32[]{:S(2)}) copy-start(f32[16,2]{0,1:T(2,128)} %param.13) | copy-start | bytes 388
  18.0 12.8 %collective-permute-start.6 = (f32[3,16,14,3]{3,1,2,0:T(8,128)S(1)}, f32[3,16,14,3]{3,1,2,0:T(8,128)S(1)}, u32[]{:S(2)}, u32[]{:S(2)}) collective-permute-start(f32[3,16,14,3]{3,1,2,0:T(8,128)S(1)} %get-tuple-element.20), channel_id=1, source_target_pairs={{0,1},{1,2},{2,3},{3,0},{4,5},{5,6},{6,7},{7,4},{8,9},{9,10},{10,1... | collective-permute-start | bytes 24200 | tf_op jit(solution)/shard_map/ppermute | solution.py:31
  19.6 15.5 %collective-permute-start.5 = (f32[3,16,14,3]{3,1,2,0:T(8,128)S(1)}, f32[3,16,14,3]{3,1,2,0:T(8,128)S(1)}, u32[]{:S(2)}, u32[]{:S(2)}) collective-permute-start(f32[3,16,14,3]{3,1,2,0:T(8,128)S(1)} %get-tuple-element.19), channel_id=1, source_target_pairs={{1,0},{2,1},{3,2},{0,3},{5,4},{6,5},{7,6},{4,7},{9,8},{10,9},{11,1... | collective-permute-start | bytes 24200 | tf_op jit(solution)/shard_map/ppermute | solution.py:33
  22.6 3.9 %collective-permute-start.2 = (f32[2,3,8,128]{3,0,2,1:T(2,128)S(1)}, f32[2,3,8,128]{3,0,2,1:T(2,128)S(1)}, u32[]{:S(2)}, u32[]{:S(2)}) collective-permute-start(f32[2,3,8,128]{3,0,2,1:T(2,128)S(1)} %convolution_bitcast_fusion.6), channel_id=1, source_target_pairs={{0,16},{16,0},{1,17},{17,1},{2,18},{18,2},{3,19},{19,3},{4,20},{20... | collective-permute-start | bytes 73736 | tf_op jit(solution)/shard_map/ppermute | solution.py:18
  37.1 8.8 %collective-permute-start.8 = (f32[3,2,8,128]{3,1,2,0:T(2,128)S(1)}, f32[3,2,8,128]{3,1,2,0:T(2,128)S(1)}, u32[]{:S(2)}, u32[]{:S(2)}) collective-permute-start(f32[3,2,8,128]{3,1,2,0:T(2,128)S(1)} %get-tuple-element.42), channel_id=1, source_target_pairs={{0,16},{1,17},{2,18},{3,19},{4,20},{5,21},{6,22},{7,23},{8,24},{9,... | collective-permute-start | bytes 73736 | tf_op jit(solution)/shard_map/ppermute | solution.py:31
  40.7 5.7 %collective-permute-start.7 = (f32[3,2,8,128]{3,1,2,0:T(2,128)S(1)}, f32[3,2,8,128]{3,1,2,0:T(2,128)S(1)}, u32[]{:S(2)}, u32[]{:S(2)}) collective-permute-start(f32[3,2,8,128]{3,1,2,0:T(2,128)S(1)} %get-tuple-element.41), channel_id=1, source_target_pairs={{16,0},{17,1},{18,2},{19,3},{20,4},{21,5},{22,6},{23,7},{24,8},{25... | collective-permute-start | bytes 73736 | tf_op jit(solution)/shard_map/ppermute | solution.py:33
  44.1 7.3 %collective-permute-start.11 = (f32[3,16,3,128]{3,1,2,0:T(8,128)S(1)}, f32[3,16,3,128]{3,1,2,0:T(8,128)S(1)}, u32[]{:S(2)}, u32[]{:S(2)}) collective-permute-start(f32[3,16,3,128]{3,1,2,0:T(8,128)S(1)} %get-tuple-element.38), channel_id=1, source_target_pairs={{0,4},{4,8},{8,12},{12,0},{1,5},{5,9},{9,13},{13,1},{2,6},{6,10},{... | collective-permute-start | bytes 221192 | tf_op jit(solution)/shard_map/ppermute | solution.py:31
  44.1 7.2 %collective-permute-start.10 = (f32[3,16,3,128]{3,1,2,0:T(8,128)S(1)}, f32[3,16,3,128]{3,1,2,0:T(8,128)S(1)}, u32[]{:S(2)}, u32[]{:S(2)}) collective-permute-start(f32[3,16,3,128]{3,1,2,0:T(8,128)S(1)} %get-tuple-element.37), channel_id=1, source_target_pairs={{4,0},{8,4},{12,8},{0,12},{5,1},{9,5},{13,9},{1,13},{6,2},{10,6},{... | collective-permute-start | bytes 221192 | tf_op jit(solution)/shard_map/ppermute | solution.py:33
  47.1 3.9 %collective-permute-start.9 = (f32[2,3,8,128]{3,0,2,1:T(2,128)S(1)}, f32[2,3,8,128]{3,0,2,1:T(2,128)S(1)}, u32[]{:S(2)}, u32[]{:S(2)}) collective-permute-start(f32[2,3,8,128]{3,0,2,1:T(2,128)S(1)} %convolution_bitcast_fusion.5), channel_id=1, source_target_pairs={{0,16},{16,0},{1,17},{17,1},{2,18},{18,2},{3,19},{19,3},{4,20},{20... | collective-permute-start | bytes 73736 | tf_op jit(solution)/shard_map/ppermute | solution.py:18
  51.6 12.8 %collective-permute-start.13 = (f32[3,16,14,3]{3,1,2,0:T(8,128)S(1)}, f32[3,16,14,3]{3,1,2,0:T(8,128)S(1)}, u32[]{:S(2)}, u32[]{:S(2)}) collective-permute-start(f32[3,16,14,3]{3,1,2,0:T(8,128)S(1)} %get-tuple-element.18), channel_id=1, source_target_pairs={{0,1},{1,2},{2,3},{3,0},{4,5},{5,6},{6,7},{7,4},{8,9},{9,10},{10,1... | collective-permute-start | bytes 24200 | tf_op jit(solution)/shard_map/ppermute | solution.py:31
  52.8 15.1 %collective-permute-start.12 = (f32[3,16,14,3]{3,1,2,0:T(8,128)S(1)}, f32[3,16,14,3]{3,1,2,0:T(8,128)S(1)}, u32[]{:S(2)}, u32[]{:S(2)}) collective-permute-start(f32[3,16,14,3]{3,1,2,0:T(8,128)S(1)} %get-tuple-element.17), channel_id=1, source_target_pairs={{1,0},{2,1},{3,2},{0,3},{5,4},{6,5},{7,6},{4,7},{9,8},{10,9},{11,1... | collective-permute-start | bytes 24200 | tf_op jit(solution)/shard_map/ppermute | solution.py:33
  72.9 3.9 %collective-permute-start.14 = (f32[2,3,8,128]{3,0,2,1:T(2,128)S(1)}, f32[2,3,8,128]{3,0,2,1:T(2,128)S(1)}, u32[]{:S(2)}, u32[]{:S(2)}) collective-permute-start(f32[2,3,8,128]{3,0,2,1:T(2,128)S(1)} %convolution_bitcast_fusion.4), channel_id=1, source_target_pairs={{0,16},{16,0},{1,17},{17,1},{2,18},{18,2},{3,19},{19,3},{4,20},{20... | collective-permute-start | bytes 73736 | tf_op jit(solution)/shard_map/ppermute | solution.py:18
  74.8 8.0 %collective-permute-start.17 = (f32[6,16,3,128]{3,1,2,0:T(8,128)S(1)}, f32[6,16,3,128]{3,1,2,0:T(8,128)S(1)}, u32[]{:S(2)}, u32[]{:S(2)}) collective-permute-start(f32[6,16,3,128]{3,1,2,0:T(8,128)S(1)} %get-tuple-element.16), channel_id=1, source_target_pairs={{4,0},{8,4},{12,8},{0,12},{5,1},{9,5},{13,9},{1,13},{6,2},{10,6},{... | collective-permute-start | bytes 442376 | tf_op jit(solution)/shard_map/ppermute | solution.py:33
  74.8 7.9 %collective-permute-start.18 = (f32[6,16,3,128]{3,1,2,0:T(8,128)S(1)}, f32[6,16,3,128]{3,1,2,0:T(8,128)S(1)}, u32[]{:S(2)}, u32[]{:S(2)}) collective-permute-start(f32[6,16,3,128]{3,1,2,0:T(8,128)S(1)} %get-tuple-element.15), channel_id=1, source_target_pairs={{0,4},{4,8},{8,12},{12,0},{1,5},{5,9},{9,13},{13,1},{2,6},{6,10},{... | collective-permute-start | bytes 442376 | tf_op jit(solution)/shard_map/ppermute | solution.py:31
  77.6 16.6 %collective-permute-start.16 = (f32[3,2,8,128]{3,1,2,0:T(2,128)S(1)}, f32[3,2,8,128]{3,1,2,0:T(2,128)S(1)}, u32[]{:S(2)}, u32[]{:S(2)}) collective-permute-start(f32[3,2,8,128]{3,1,2,0:T(2,128)S(1)} %get-tuple-element.34), channel_id=1, source_target_pairs={{0,16},{1,17},{2,18},{3,19},{4,20},{5,21},{6,22},{7,23},{8,24},{9,... | collective-permute-start | bytes 73736 | tf_op jit(solution)/shard_map/ppermute | solution.py:31
  81.2 12.9 %collective-permute-start.15 = (f32[3,2,8,128]{3,1,2,0:T(2,128)S(1)}, f32[3,2,8,128]{3,1,2,0:T(2,128)S(1)}, u32[]{:S(2)}, u32[]{:S(2)}) collective-permute-start(f32[3,2,8,128]{3,1,2,0:T(2,128)S(1)} %get-tuple-element.33), channel_id=1, source_target_pairs={{16,0},{17,1},{18,2},{19,3},{20,4},{21,5},{22,6},{23,7},{24,8},{25... | collective-permute-start | bytes 73736 | tf_op jit(solution)/shard_map/ppermute | solution.py:33
  83.8 7.7 %collective-permute-start.20 = (f32[6,16,14,3]{2,1,3,0:T(8,128)S(1)}, f32[6,16,14,3]{2,1,3,0:T(8,128)S(1)}, u32[]{:S(2)}, u32[]{:S(2)}) collective-permute-start(f32[6,16,14,3]{2,1,3,0:T(8,128)S(1)} %copy.97), channel_id=1, source_target_pairs={{0,1},{1,2},{2,3},{3,0},{4,5},{5,6},{6,7},{7,4},{8,9},{9,10},{10,1... | collective-permute-start | bytes 48392 | tf_op jit(solution)/shard_map/ppermute | solution.py:31
  85.3 9.5 %copy-start.3 = (f32[16,8,128]{2,0,1:T(8,128)S(1)}, f32[16,8,128]{2,0,1:T(8,128)}, u32[]{:S(2)}) copy-start(f32[16,8,128]{2,0,1:T(8,128)} %copy.104) | copy-start | bytes 196612
  85.3 9.5 %copy-start.10 = (s32[8]{0:T(128)S(1)}, s32[8]{0:T(128)}, u32[]{:S(2)}) copy-start(s32[8]{0:T(128)} %copy-done.9) | copy-start | bytes 100
  85.3 9.5 %copy-start.12 = (pred[8]{0:T(512)(128)(4,1)S(1)}, pred[8]{0:T(512)(128)(4,1)}, u32[]{:S(2)}) copy-start(pred[8]{0:T(512)(128)(4,1)} %copy-done.11) | copy-start | bytes 28
  85.3 7.2 %collective-permute-start.19 = (f32[6,16,14,3]{2,1,3,0:T(8,128)S(1)}, f32[6,16,14,3]{2,1,3,0:T(8,128)}, u32[]{:S(2)}, u32[]{:S(2)}) collective-permute-start(f32[6,16,14,3]{2,1,3,0:T(8,128)S(1)} %copy.95), channel_id=1, source_target_pairs={{1,0},{2,1},{3,2},{0,3},{5,4},{6,5},{7,6},{4,7},{9,8},{10,9},{11,1... | collective-permute-start | bytes 48392 | tf_op jit(solution)/shard_map/ppermute | solution.py:33
  94.1 0.6 copy-start.14
  94.2 0.6 copy-start.15
  94.8 2.8 %copy-start.8 = (f32[4,4]{1,0:T(4,128)S(1)}, f32[4,4]{1,0:T(4,128)}, u32[]{:S(2)}) copy-start(f32[4,4]{1,0:T(4,128)} %param.14) | copy-start | bytes 196
  97.9 4.2 %collective-permute-start.21 = (f32[2,3,8,128]{3,0,2,1:T(2,128)S(1)}, f32[2,3,8,128]{3,0,2,1:T(2,128)S(1)}, u32[]{:S(2)}, u32[]{:S(2)}) collective-permute-start(f32[2,3,8,128]{3,0,2,1:T(2,128)S(1)} %convolution_bitcast_fusion.3), channel_id=1, source_target_pairs={{0,16},{16,0},{1,17},{17,1},{2,18},{18,2},{3,19},{19,3},{4,20},{20... | collective-permute-start | bytes 73736 | tf_op jit(solution)/shard_map/ppermute | solution.py:18
  100.4 9.0 %collective-permute-start.24 = (f32[6,16,3,128]{3,1,2,0:T(8,128)S(1)}, f32[6,16,3,128]{3,1,2,0:T(8,128)S(1)}, u32[]{:S(2)}, u32[]{:S(2)}) collective-permute-start(f32[6,16,3,128]{3,1,2,0:T(8,128)S(1)} %get-tuple-element.12), channel_id=1, source_target_pairs={{4,0},{8,4},{12,8},{0,12},{5,1},{9,5},{13,9},{1,13},{6,2},{10,6},{... | collective-permute-start | bytes 442376 | tf_op jit(solution)/shard_map/ppermute | solution.py:33
  100.4 9.0 %collective-permute-start.25 = (f32[6,16,3,128]{3,1,2,0:T(8,128)S(1)}, f32[6,16,3,128]{3,1,2,0:T(8,128)S(1)}, u32[]{:S(2)}, u32[]{:S(2)}) collective-permute-start(f32[6,16,3,128]{3,1,2,0:T(8,128)S(1)} %get-tuple-element.11), channel_id=1, source_target_pairs={{0,4},{4,8},{8,12},{12,0},{1,5},{5,9},{9,13},{13,1},{2,6},{6,10},{... | collective-permute-start | bytes 442376 | tf_op jit(solution)/shard_map/ppermute | solution.py:31
  102.9 9.8 %copy-start.2 = (f32[3,16,8,128]{3,1,2,0:T(8,128)}, f32[3,16,8,128]{3,1,2,0:T(8,128)S(1)}, u32[]{:S(2)}) copy-start(f32[3,16,8,128]{3,1,2,0:T(8,128)S(1)} %fusion.5) | copy-start | bytes 589828
  103.5 17.6 %collective-permute-start.23 = (f32[3,2,8,128]{3,1,2,0:T(2,128)}, f32[3,2,8,128]{3,1,2,0:T(2,128)}, u32[]{:S(2)}, u32[]{:S(2)}) collective-permute-start(f32[3,2,8,128]{3,1,2,0:T(2,128)} %get-tuple-element.27), channel_id=1, source_target_pairs={{0,16},{1,17},{2,18},{3,19},{4,20},{5,21},{6,22},{7,23},{8,24},{9,... | collective-permute-start | bytes 73736 | tf_op jit(solution)/shard_map/ppermute | solution.py:31
  108.1 13.1 %collective-permute-start.22 = (f32[3,2,8,128]{3,1,2,0:T(2,128)}, f32[3,2,8,128]{3,1,2,0:T(2,128)}, u32[]{:S(2)}, u32[]{:S(2)}) collective-permute-start(f32[3,2,8,128]{3,1,2,0:T(2,128)} %get-tuple-element.26), channel_id=1, source_target_pairs={{16,0},{17,1},{18,2},{19,3},{20,4},{21,5},{22,6},{23,7},{24,8},{25... | collective-permute-start | bytes 73736 | tf_op jit(solution)/shard_map/ppermute | solution.py:33
  111.1 7.3 %collective-permute-start.27 = (f32[6,16,14,3]{2,1,3,0:T(8,128)}, f32[6,16,14,3]{2,1,3,0:T(8,128)S(1)}, u32[]{:S(2)}, u32[]{:S(2)}) collective-permute-start(f32[6,16,14,3]{2,1,3,0:T(8,128)} %copy.108), channel_id=1, source_target_pairs={{0,1},{1,2},{2,3},{3,0},{4,5},{5,6},{6,7},{7,4},{8,9},{9,10},{10,1... | collective-permute-start | bytes 48392 | tf_op jit(solution)/shard_map/ppermute | solution.py:31
  112.7 6.9 %collective-permute-start.26 = (f32[6,16,14,3]{2,1,3,0:T(8,128)S(1)}, f32[6,16,14,3]{2,1,3,0:T(8,128)}, u32[]{:S(2)}, u32[]{:S(2)}) collective-permute-start(f32[6,16,14,3]{2,1,3,0:T(8,128)S(1)} %copy.106), channel_id=1, source_target_pairs={{1,0},{2,1},{3,2},{0,3},{5,4},{6,5},{7,6},{4,7},{9,8},{10,9},{11,1... | collective-permute-start | bytes 48392 | tf_op jit(solution)/shard_map/ppermute | solution.py:33
